TPU v7x, 32 devices: a whole 2x2x4 slice. The times are simulated.
32 devices in a mesh: list: 8 (over y, x, core), shard: 4 (over z).
Axes of the slice: x: 2, y: 2, z: 4, core: 2. Of those that a mesh axis runs over, the one named last changes fastest.
Arguments:
- features: bfloat16 [256, 4096], P(('list', 'shard')), may hold values from -6 to 6
- norm_gain: float32 [4096], replicated, may hold values from 0.5 to 1.5
- gate_weight: bfloat16 [4096, 11008], P('shard', 'list'), may hold values from -0.09375 to 0.09375
- up_weight: bfloat16 [4096, 11008], P('shard', 'list'), may hold values from -0.09375 to 0.09375
- down_weight: bfloat16 [11008, 4096], P('list', 'shard'), may hold values from -0.0546875 to 0.0546875
- centroids: float32 [16, 4096], P('list'), may hold values from -6 to 6
- list_ids: int32 [256], P(('list', 'shard')), may hold values from 0 to 15
- live: int32 [256], P(('list', 'shard')), may hold values 0 or 1
Outputs:
- residuals: bfloat16 [256, 4096], P(('list', 'shard'))
- refreshed: float32 [16, 4096], P('list')
All inputs are finite; a program needn't handle non-finite values. No bound on the sum of `live` on one device may be relied on, other than what follows from the above.
Results may differ from a plain program's by a relative error of at most 0.015.
Values may be sent and summed in bfloat16 or wider, within the bound.
A program may use at most 64 MiB of HBM per device.

v0:
```python
import jax
import jax.numpy as jnp
from jax import lax
from jax.sharding import PartitionSpec as P


def body(features, norm_gain, gate_weight, up_weight, down_weight, centroids, list_ids, live):
    local_rows = features.shape[0]
    width = features.shape[1]
    group_rows = lax.all_gather(features, "list", axis=0, tiled=True)
    first = jnp.dot(
        group_rows,
        lax.all_gather(gate_weight, "shard", axis=0, tiled=True),
        preferred_element_type=jnp.float32,
    )
    second = jnp.dot(
        group_rows,
        lax.all_gather(up_weight, "shard", axis=0, tiled=True),
        preferred_element_type=jnp.float32,
    )
    hidden = (jax.nn.silu(first) * second).astype(jnp.bfloat16)
    shard_count = lax.axis_size("shard")
    column_width = down_weight.shape[1]
    column_terms = jnp.dot(
        lax.all_gather(hidden, "shard", axis=0, tiled=True),
        down_weight,
        preferred_element_type=jnp.float32,
    )
    column_terms = column_terms.reshape(shard_count, hidden.shape[0], column_width)
    column_part = lax.psum_scatter(
        column_terms.astype(jnp.bfloat16), "list", scatter_dimension=1, tiled=True
    ).astype(jnp.float32)
    mixed = (
        lax.all_to_all(
            column_part.astype(jnp.bfloat16), "shard", split_axis=0, concat_axis=2, tiled=True
        )
        .astype(column_part.dtype)
        .reshape(local_rows, width)
    )
    stream = features.astype(jnp.float32) + mixed
    scale = lax.rsqrt(jnp.mean(stream * stream, axis=1, keepdims=True) + 1e-05)
    embedding = (stream * scale * norm_gain).astype(jnp.bfloat16)
    table = lax.all_gather(centroids.astype(jnp.bfloat16), "list", axis=0, tiled=True)
    list_total = table.shape[0]
    alive = live.astype(jnp.float32)
    member = (list_ids[:, None] == jnp.arange(list_total, dtype=jnp.int32)[None, :]).astype(
        jnp.float32
    )
    picked = jnp.dot(member.astype(jnp.bfloat16), table, preferred_element_type=jnp.float32)
    residuals = (alive[:, None] * (embedding.astype(jnp.float32) - picked)).astype(jnp.bfloat16)
    weighted = member * alive[:, None]
    dense_sums = jnp.dot(weighted.T, embedding.astype(jnp.float32), precision=lax.Precision.HIGHEST)
    dense_counts = jnp.sum(weighted, axis=0)
    owned_sums, owned_counts = (
        lax.psum_scatter(
            dense_sums.astype(jnp.bfloat16), "list", scatter_dimension=0, tiled=True
        ).astype(jnp.float32),
        lax.psum_scatter(
            dense_counts.astype(jnp.bfloat16), "list", scatter_dimension=0, tiled=True
        ).astype(jnp.float32),
    )
    total_sums, total_counts = (
        lax.psum(owned_sums.astype(jnp.bfloat16), "shard").astype(jnp.float32),
        lax.psum(owned_counts.astype(jnp.bfloat16), "shard").astype(jnp.float32),
    )
    refreshed = (centroids + total_sums) / (1.0 + total_counts[:, None])
    return (residuals, refreshed)


def solution(mesh):
    in_specs = (
        P(("list", "shard"), None),
        P(),
        P("shard", "list"),
        P("shard", "list"),
        P("list", "shard"),
        P("list", None),
        P(("list", "shard")),
        P(("list", "shard")),
    )
    out_specs = (P(("list", "shard"), None), P("list", None))
    return jax.shard_map(body, mesh=mesh, in_specs=in_specs, out_specs=out_specs, check_vma=False)
```

profile of v0, /device:TPU:0, one launch (start us, length us, event | category | flops | bytes accessed | tf_op | source)
XLA Modules:
  0.0 567.5 jit_solution(15856995516734702170)
XLA Ops:
  7.2 0.0 copy-start
  7.2 0.0 all-gather.4.cloned.1.call-start
  7.2 0.7 all-gather.4.cloned.1.call-update
  7.9 0.0 all-gather.6.cloned.1.call-start
  8.0 0.7 all-gather.6.cloned.1.call-update
  8.7 0.0 reduce-scatter.4.cloned.1.call-start
  8.7 11.6 %all_gather.15 = bf16[64,4096]{1,0:T(8,128)(2,1)S(1)} all-gather(bf16[8,4096]{1,0:T(8,128)(2,1)} %param.8), channel_id=1, replica_groups=mesh['list'=8,'shard'=4] {'list'}, dimensions={0}, use_global_device_ids=true | all-gather | bytes 589824 | tf_op jit(solution)/shard_map/all_gather | solution.py:10
  20.3 188.7 %all-gather.4.cloned.1.call-done = bf16[4096,1376]{0,1:T(8,128)(2,1)} async-done(((bf16[1024,1376]{0,1:T(8,128)(2,1)}), bf16[4096,1376]{0,1:T(8,128)(2,1)}) %all-gather.4.cloned.1.call-update) | async-done | bytes 11272208 | tf_op jit(solution)/shard_map/all_gather | solution.py:13
  209.1 8.4 %fusion.9 = f32[64,1376]{1,0:T(8,128)} fusion(bf16[64,4096]{1,0:T(8,128)(2,1)S(1)} %all_gather.15, bf16[4096,1376]{0,1:T(8,128)(2,1)} %all-gather.4.cloned.1.call-done), kind=kOutput, calls=%fused_computation.25 | convolution fusion | flops 721420288 | bytes 12148736 | tf_op jit(solution)/shard_map/dot_general | solution.py:11
  217.5 0.0 copy-start.5
  217.5 0.0 copy-start.1
  217.5 0.0 copy-start.6
  217.5 0.0 copy-start.2
  217.5 188.1 %all-gather.6.cloned.1.call-done = bf16[4096,1376]{0,1:T(8,128)(2,1)} async-done(((bf16[1024,1376]{0,1:T(8,128)(2,1)}), bf16[4096,1376]{0,1:T(8,128)(2,1)}) %all-gather.6.cloned.1.call-update) | async-done | bytes 11272208 | tf_op jit(solution)/shard_map/all_gather | solution.py:18
  405.6 7.7 %fusion.2 = bf16[64,1376]{1,0:T(8,128)(2,1)S(1)} fusion(bf16[64,4096]{1,0:T(8,128)(2,1)S(1)} %all_gather.15, bf16[4096,1376]{0,1:T(8,128)(2,1)} %all-gather.6.cloned.1.call-done, f32[64,1376]{1,0:T(8,128)} %fusion.9), kind=kOutput, calls=%fused_computation.5 | convolution fusion | flops 721948672 | bytes 12324864 | tf_op jit(solution)/shard_map/dot_general | solution.py:16
  413.3 17.3 %all_gather.18 = bf16[256,1376]{1,0:T(8,128)(2,1)S(1)} all-gather(bf16[64,1376]{1,0:T(8,128)(2,1)S(1)} %fusion.2), channel_id=1, replica_groups=mesh['list'=8,'shard'=4] {'shard'}, dimensions={0}, use_global_device_ids=true | all-gather | bytes 880640 | tf_op jit(solution)/shard_map/all_gather | solution.py:25
  430.6 0.0 copy-done
  430.6 1.0 convolution_convert_fusion.1
  431.6 0.4 copy.10
  432.0 1.0 copy.12
  432.9 0.0 reduce-scatter.4.cloned.1.call-update
  433.0 33.7 %reduce-scatter.4.cloned.1.call-done = bf16[8,4096]{1,0:T(8,128)(2,1)} async-done(((bf16[64,4096]{1,0:T(8,128)(2,1)}), bf16[8,4096]{1,0:T(8,128)(2,1)}) %reduce-scatter.4.cloned.1.call-update) | async-done | bytes 65552
  466.6 0.9 reshape.33
  467.5 0.7 copy.11
  468.2 4.6 all-to-all-start
  472.8 0.0 all-reduce.5.cloned.1.call-start
  472.8 0.0 copy-done.5
  472.8 5.7 %all-to-all-done = bf16[4,8,1024]{2,1,0:T(8,128)(2,1)S(1)} async-done(((bf16[4,8,1024]{2,1,0:T(8,128)(2,1)}), bf16[4,8,1024]{2,1,0:T(8,128)(2,1)S(1)}, u32[]{:S(2)}, u32[]{:S(2)}) %all-to-all-start) | async-done | bytes 65568 | tf_op jit(solution)/shard_map/all_to_all | solution.py:34
  478.5 0.0 copy-done.1
  478.5 0.2 multiply_reduce_fusion
  478.7 0.0 copy-done.3
  478.7 0.1 multiply_convert_fusion
  478.8 0.0 copy-done.4
  478.8 1.0 convolution_convert_fusion
  479.8 0.0 all-reduce.5.cloned.1.call-update
  479.9 0.1 select_reduce_fusion
  479.9 11.9 %all-reduce.1 = bf16[16]{0:T(256)(128)(2,1)S(1)} all-reduce(bf16[16]{0:T(256)(128)(2,1)S(1)} %select_reduce_fusion), channel_id=4, replica_groups=mesh['list'=8,'shard'=4] {'list'}, use_global_device_ids=true, to_apply=%region_5.6.clone | all-reduce | flops 16 | bytes 64
  491.8 0.0 copy-done.6
  491.8 0.6 dynamic-slice
  493.0 0.1 dynamic-slice.3
  493.1 37.9 %all-reduce.5.cloned.1.call-done = bf16[16,4096]{1,0:T(8,128)(2,1)} async-done(((bf16[16,4096]{1,0:T(8,128)(2,1)}), bf16[16,4096]{1,0:T(8,128)(2,1)}) %all-reduce.5.cloned.1.call-update) | async-done | bytes 131088
  531.1 0.9 constant_dynamic-slice_fusion
  531.9 18.9 %all-reduce.2 = (bf16[2,4096]{1,0:T(2,128)(2,1)S(1)}, bf16[2]{0:T(256)(128)(2,1)S(1)}) all-reduce(bf16[2,4096]{1,0:T(2,128)(2,1)S(1)} %constant_dynamic-slice_fusion, bf16[2]{0:T(256)(128)(2,1)S(1)} %dynamic-slice.3), channel_id=1, replica_groups=mesh['list'=8,'shard'=4] {'shard'}, use_global_device_ids=true, to_apply=%region_3.4 | all-reduce | flops 8194 | bytes 32776 | tf_op jit(solution)/shard_map/psum | solution.py:63
  550.8 0.0 copy-done.2
  550.8 0.7 add_divide_fusion
  551.5 8.5 %all-gather = bf16[8,2,4096]{2,1,0:T(2,128)(2,1)S(1)} all-gather(bf16[1,2,4096]{2,1,0:T(2,128)(2,1)S(1)} %get-tuple-element.5), channel_id=1, replica_groups=mesh['list'=8,'shard'=4] {'list'}, dimensions={0}, use_global_device_ids=true | all-gather | bytes 147456 | tf_op jit(solution)/shard_map/all_gather | solution.py:43
  560.1 0.1 reshape.31
  560.1 0.8 fusion.1
  (6 shorter events, 0.0 us)
Async XLA Ops:
  7.2 423.4 %copy-start = (bf16[1376,1024]{1,0:T(8,128)(2,1)S(1)}, bf16[1376,1024]{1,0:T(8,128)(2,1)}, u32[]{:S(2)}) copy-start(bf16[1376,1024]{1,0:T(8,128)(2,1)} %param.12) | copy-start | bytes 8454148
  7.2 201.9 %all-gather.4.cloned.1.call-start = ((), (), s32[]{:S(2)}) async-start(), calls=%async_computation.2 | async-start | bytes 14090240 | tf_op jit(solution)/shard_map/all_gather | solution.py:13
  7.9 397.7 %all-gather.6.cloned.1.call-start = ((), (), s32[]{:S(2)}) async-start(), calls=%async_computation.3 | async-start | bytes 14090240 | tf_op jit(solution)/shard_map/all_gather | solution.py:18
  8.7 458.0 %reduce-scatter.4.cloned.1.call-start = ((), (), s32[]{:S(2)}) async-start(), calls=%async_computation.4 | async-start | bytes 589824
  217.5 255.3 %copy-start.5 = (s32[8]{0:T(128)S(1)}, s32[8]{0:T(128)}, u32[]{:S(2)}) copy-start(s32[8]{0:T(128)} %param.15) | copy-start | bytes 100
  217.5 261.1 %copy-start.1 = (bf16[8,4096]{1,0:T(8,128)(2,1)S(1)}, bf16[8,4096]{1,0:T(8,128)(2,1)}, u32[]{:S(2)}) copy-start(bf16[8,4096]{1,0:T(8,128)(2,1)} %param.8) | copy-start | bytes 196612
  217.5 261.2 %copy-start.3 = (f32[4096]{0:T(1024)S(1)}, f32[4096]{0:T(1024)}, u32[]{:S(2)}) copy-start(f32[4096]{0:T(1024)} %param.9) | copy-start | bytes 49156
  217.5 261.3 %copy-start.4 = (s32[8]{0:T(128)S(1)}, s32[8]{0:T(128)}, u32[]{:S(2)}) copy-start(s32[8]{0:T(128)} %param.14) | copy-start | bytes 100
  217.5 274.3 %copy-start.6 = (u32[32]{0:T(128)S(1)}, u32[32]{0:T(128)}, u32[]{:S(2)}) copy-start(u32[32]{0:T(128)} %constant.18) | copy-start | bytes 388
  217.5 333.3 %copy-start.2 = (f32[2,4096]{1,0:T(2,128)S(1)}, f32[2,4096]{1,0:T(2,128)}, u32[]{:S(2)}) copy-start(f32[2,4096]{1,0:T(2,128)} %param.13) | copy-start | bytes 98308
  468.2 10.3 %all-to-all-start = ((bf16[4,8,1024]{2,1,0:T(8,128)(2,1)}), bf16[4,8,1024]{2,1,0:T(8,128)(2,1)S(1)}, u32[]{:S(2)}, u32[]{:S(2)}) async-start(bf16[4,8,1024]{2,1,0:T(8,128)(2,1)} %copy.11), calls=%async_computation | async-start | bytes 131072 | tf_op jit(solution)/shard_map/all_to_all | solution.py:34
  472.8 58.3 %all-reduce.5.cloned.1.call-start = ((), (), s32[]{:S(2)}) async-start(), calls=%async_computation.5 | async-start | bytes 262144
Sparse Core Ops, SparseCore 0:
  9.6 199.4 all-gather.3
  210.6 194.9 all-gather.5
  433.1 33.5 reduce-scatter.3
  480.0 51.0 all-reduce.4
where the time goes:
time: 568 us
  waiting for transfers between devices  456 us (80%)
  blocking collectives  68.2 us (12%)
  matrix products  18.9 us (3%)
  between operations  14.5 us (3%)
    all_gather x1, waiting for transfers between devices, body(): lax.all_gather(gate_weight, 'shard', axis=0, tiled=True)  189 us
    all_gather x1, waiting for transfers between devices, body(): lax.all_gather(up_weight, 'shard', axis=0, tiled=True)  188 us
    unnamed x6, waiting for transfers between devices  73 us
    psum x1, blocking collectives, body(): lax.psum(owned_sums.astype(jnp.bfloat16), 'shard').astype(jnp.float32)  18.9 us
    all_gather x1, blocking collectives, body(): lax.all_gather(hidden, 'shard', axis=0, tiled=True)  17.3 us
    unnamed x1, blocking collectives  11.9 us
    all_gather x1, blocking collectives, body(): group_rows = lax.all_gather(features, 'list', axis=0, tiled=True)  11.6 us
  transfers between devices with their start and end apart: 5, of which 5 were waited for; matrix products, arithmetic and copies ran while one was open for 2% of the time, Pallas kernels for 0%

commit v1 on v0

v1 whole, which is shorter than its diff:
```python
import jax
import jax.numpy as jnp
from jax import lax
from jax.sharding import PartitionSpec as P


def body(features, norm_gain, gate_weight, up_weight, down_weight, centroids, list_ids, live):
    width = features.shape[1]
    own_lists = centroids.shape[0]
    column_width = down_weight.shape[1]
    me_list, me_shard = lax.axis_index("list"), lax.axis_index("shard")
    group = lax.all_to_all(features, "shard", split_axis=1, concat_axis=0, tiled=True)
    rows = lax.all_gather(group, "list", axis=0, tiled=True)
    ids_live = lax.all_gather(
        jnp.stack([list_ids, live], axis=1), ("list", "shard"), axis=0, tiled=True
    )
    first = jnp.dot(rows, gate_weight, preferred_element_type=jnp.float32).astype(jnp.bfloat16)
    second = jnp.dot(rows, up_weight, preferred_element_type=jnp.float32).astype(jnp.bfloat16)
    both = lax.psum_scatter(
        jnp.concatenate([first, second], axis=1), "shard", scatter_dimension=0, tiled=True
    ).astype(jnp.float32)
    half = gate_weight.shape[1]
    hidden = (jax.nn.silu(both[:, :half]) * both[:, half:]).astype(jnp.bfloat16)
    hidden = lax.all_gather(hidden, "shard", axis=0, tiled=True)
    terms = jnp.dot(hidden, down_weight, preferred_element_type=jnp.float32)
    part = lax.psum_scatter(
        terms.astype(jnp.bfloat16), "list", scatter_dimension=0, tiled=True
    ).astype(jnp.float32)
    stream = group.astype(jnp.float32) + part
    squares = lax.psum(jnp.sum(stream * stream, axis=1, keepdims=True), "shard")
    scale = lax.rsqrt(squares / width + 1e-05)
    gain = lax.dynamic_slice_in_dim(norm_gain, me_shard * column_width, column_width, 0)
    embedding = (stream * scale * gain).astype(jnp.bfloat16)
    table = lax.all_gather(centroids.astype(jnp.bfloat16), "list", axis=0, tiled=True)
    table = lax.dynamic_slice_in_dim(table, me_shard * column_width, column_width, 1)
    list_total = table.shape[0]
    member = (
        ids_live[:, :1] == jnp.arange(list_total, dtype=jnp.int32)[None, :]
    ).astype(jnp.float32)
    alive = ids_live[:, 1:].astype(jnp.float32)
    weighted = member * alive
    count = lax.dynamic_slice_in_dim(jnp.sum(weighted, axis=0), me_list * own_lists, own_lists, 0)
    group_rows = group.shape[0]
    member = lax.dynamic_slice_in_dim(member, me_list * group_rows, group_rows, 0)
    weighted = lax.dynamic_slice_in_dim(weighted, me_list * group_rows, group_rows, 0)
    alive = lax.dynamic_slice_in_dim(alive, me_list * group_rows, group_rows, 0)
    picked = jnp.dot(member.astype(jnp.bfloat16), table, preferred_element_type=jnp.float32)
    residuals = (alive * (embedding.astype(jnp.float32) - picked)).astype(jnp.bfloat16)
    residuals = lax.all_to_all(residuals, "shard", split_axis=0, concat_axis=1, tiled=True)
    sums = jnp.dot(
        weighted.T.astype(jnp.bfloat16), embedding, preferred_element_type=jnp.float32
    )
    sums = lax.psum_scatter(sums, "list", scatter_dimension=0, tiled=True)
    sums = lax.all_gather(sums, "shard", axis=1, tiled=True)
    refreshed = (centroids + sums) / (1.0 + count[:, None])
    return (residuals, refreshed)


def solution(mesh):
    in_specs = (
        P(("list", "shard"), None),
        P(),
        P("shard", "list"),
        P("shard", "list"),
        P("list", "shard"),
        P("list", None),
        P(("list", "shard")),
        P(("list", "shard")),
    )
    out_specs = (P(("list", "shard"), None), P("list", None))
    return jax.shard_map(body, mesh=mesh, in_specs=in_specs, out_specs=out_specs, check_vma=False)
```

time: 568 us -> 261 us (0.46)
  waiting for transfers between devices: 456 us -> 81.4 us
  blocking collectives: 68.2 us -> 148 us
  matrix products: 18.9 us -> 6.43 us
    all_gather x2 -> x0, waiting for transfers between devices: 377 us -> none  [the longest x1 189 us: body(): lax.all_gather(gate_weight, 'shard', axis=0, tiled=True)]
    all_gather x2 -> x4, blocking collectives: 28.9 us -> 106 us  [the longest x1 65.8 us: body(): lax.all_gather(jnp.stack([list_ids, live], axis=1), ('list', 'shard'), ax...]
    reduce_scatter x0 -> x2, waiting for transfers between devices: none -> 32.1 us  [the longest x1 32.1 us: body(): lax.psum_scatter(terms.astype(jnp.bfloat16), 'list', scatter_dimension=0,...]
    unnamed x6 -> x4, waiting for transfers between devices: 73 us -> 49.3 us
    all_to_all x0 -> x2, blocking collectives: none -> 22.5 us  [the longest x1 12.4 us: body(): lax.all_to_all(features, 'shard', split_axis=1, concat_axis=0, tiled=True)]
    dot_general x4, matrix products: 18.1 us -> 5.32 us  [the longest x1 1.77 us: body(): terms = jnp.dot(hidden, down_weight, preferred_element_type=jnp.float32)]
    unnamed x1 -> x0, blocking collectives: 11.9 us -> none
    psum x1, blocking collectives: 18.9 us -> 11.7 us  [body(): squares = lax.psum(jnp.sum(stream * stream, axis=1, keepdims=True), 'shard')]
  transfers between devices with their start and end apart: 5 -> 3, of which waited for: 5 -> 2; matrix products, arithmetic and copies ran while one was open for 2% -> 1% of each run, Pallas kernels for 0% -> 0%
where the time goes in v1:
time: 261 us
  blocking collectives  148 us (57%)
  waiting for transfers between devices  81.4 us (31%)
  between operations  14.5 us (6%)
  matrix products  6.43 us (2%)
  local copies, waits for them, and re-layouts  5.48 us (2%)
  other arithmetic  4.43 us (2%)
    all_gather x1, blocking collectives, body(): lax.all_gather(jnp.stack([list_ids, live], axis=1), ('list', 'shard'), ax...  65.8 us
    unnamed x4, waiting for transfers between devices  49.3 us
    reduce_scatter x1, waiting for transfers between devices, body(): lax.psum_scatter(terms.astype(jnp.bfloat16), 'list', scatter_dimension=0,...  32.1 us
    all_gather x1, blocking collectives, body(): hidden = lax.all_gather(hidden, 'shard', axis=0, tiled=True)  16.8 us
    all_gather x1, blocking collectives, body(): sums = lax.all_gather(sums, 'shard', axis=1, tiled=True)  13.2 us
    all_to_all x1, blocking collectives, body(): lax.all_to_all(features, 'shard', split_axis=1, concat_axis=0, tiled=True)  12.4 us
    psum x1, blocking collectives, body(): squares = lax.psum(jnp.sum(stream * stream, axis=1, keepdims=True), 'shard')  11.7 us
    all_to_all x1, blocking collectives, body(): lax.all_to_all(residuals, 'shard', split_axis=0, concat_axis=1, tiled=True)  10.1 us
  transfers between devices with their start and end apart: 3, of which 2 were waited for; matrix products, arithmetic and copies ran while one was open for 1% of the time, Pallas kernels for 0%

profile of v1, /device:TPU:0, one launch (start us, length us, event | category | flops | bytes accessed | tf_op | source)
XLA Modules:
  0.0 260.8 jit_solution(7933411212026560877)
XLA Ops:
  7.2 0.0 copy-start
  7.2 0.0 reduce-scatter.7.cloned.1.call-start
  7.2 0.0 copy-start.4
  7.2 12.4 %all_to_all.38 = bf16[8,4,1024]{2,0,1:T(8,128)(2,1)S(1)} all-to-all(bf16[8,4,1024]{2,0,1:T(8,128)(2,1)} %bitcast.39), channel_id=1, replica_groups=mesh['list'=8,'shard'=4] {'shard'}, dimensions={1} | all-to-all | bytes 131072 | tf_op jit(solution)/shard_map/all_to_all | solution.py:12
  19.6 9.8 %all_gather.16 = bf16[256,1024]{1,0:T(8,128)(2,1)S(1)} all-gather(bf16[32,1024]{1,0:T(8,128)(2,1)S(1)} %bitcast.37), channel_id=1, replica_groups=mesh['list'=8,'shard'=4] {'list'}, dimensions={0}, use_global_device_ids=true | all-gather | bytes 589824 | tf_op jit(solution)/shard_map/all_gather | solution.py:13
  29.4 0.0 copy-done
  29.4 0.9 convolution_convert_fusion
  30.4 0.0 copy-done.4
  30.4 0.9 convolution_convert_fusion.1
  31.3 1.2 pad_maximum_fusion
  32.5 0.0 copy-start.2
  32.5 0.0 copy-start.3
  32.5 2.6 copy.17
  35.1 0.0 reduce-scatter.7.cloned.1.call-update
  35.1 0.0 reduce-scatter.5.cloned.1.call-start
  35.2 0.0 copy-done.2
  35.2 0.0 copy-done.3
  35.2 65.8 %all-gather = s32[32,8,2]{1,2,0:T(2,128)S(1)} all-gather(s32[1,8,2]{1,2,0:T(2,128)S(1)} %add_bitcast_fusion), channel_id=1, replica_groups=mesh['list'=8,'shard'=4] {'list','shard'}, dimensions={0}, use_global_device_ids=true | all-gather | bytes 2112 | tf_op jit(solution)/shard_map/all_gather | solution.py:14
  101.0 0.1 reshape.14
  101.1 0.7 dynamic_slice.19
  101.8 0.0 reduce-scatter.7.cloned.1.call-done
  101.8 1.2 convert_element_type.50
  103.0 0.2 fusion.3
  103.1 16.8 %all_gather.17 = bf16[256,1376]{1,0:T(8,128)(2,1)S(1)} all-gather(bf16[64,1376]{1,0:T(8,128)(2,1)S(1)} %fusion.3), channel_id=1, replica_groups=mesh['list'=8,'shard'=4] {'shard'}, dimensions={0}, use_global_device_ids=true | all-gather | bytes 880640 | tf_op jit(solution)/shard_map/all_gather | solution.py:24
  120.0 0.0 copy-done.5
  120.0 1.8 convolution_convert_fusion.2
  121.7 0.0 reduce-scatter.5.cloned.1.call-update
  121.8 0.0 all-reduce.3.cloned.1.call-start
  121.8 0.1 fusion.9
  121.9 0.1 fusion.5
  122.0 32.1 %reduce-scatter.5.cloned.1.call-done = bf16[32,1024]{1,0:T(8,128)(2,1)} async-done(((bf16[256,1024]{1,0:T(8,128)(2,1)}), bf16[32,1024]{1,0:T(8,128)(2,1)}) %reduce-scatter.5.cloned.1.call-update) | async-done | bytes 65552 | tf_op jit(solution)/shard_map/reduce_scatter | solution.py:26
  154.2 1.0 multiply_reduce_fusion
  155.1 11.7 %psum.7 = f32[32,1]{0,1:T(1,128)S(1)} all-reduce(f32[32,1]{0,1:T(1,128)S(1)} %bitcast.45), channel_id=1, replica_groups=mesh['list'=8,'shard'=4] {'shard'}, use_global_device_ids=true, to_apply=%region_3.4 | all-reduce | flops 32 | bytes 256 | tf_op jit(solution)/shard_map/psum | solution.py:30
  166.9 1.7 fusion.6
  168.5 0.0 all-reduce.3.cloned.1.call-update
  168.6 0.1 dynamic-slice_add_fusion
  168.7 0.0 copy-done.6
  168.7 0.6 dynamic-slice
  169.9 49.3 %all-reduce.3.cloned.1.call-done = f32[16,1024]{1,0:T(8,128)} async-done(((f32[16,1024]{1,0:T(8,128)}), f32[16,1024]{1,0:T(8,128)}) %all-reduce.3.cloned.1.call-update) | async-done | bytes 65552
  219.1 0.8 constant_dynamic-slice_fusion.1
  219.9 13.2 %all_gather.19 = f32[2,4096]{1,0:T(2,128)S(1)} all-gather(f32[2,1024]{1,0:T(2,128)S(1)} %constant_dynamic-slice_fusion.1), channel_id=1, replica_groups=mesh['list'=8,'shard'=4] {'shard'}, dimensions={1}, use_global_device_ids=true | all-gather | bytes 40960 | tf_op jit(solution)/shard_map/all_gather | solution.py:54
  233.1 0.0 copy-done.1
  233.1 0.7 add_divide_fusion
  233.8 8.5 %all-gather.1 = bf16[8,2,4096]{2,1,0:T(2,128)(2,1)S(1)} all-gather(bf16[1,2,4096]{2,1,0:T(2,128)(2,1)S(1)} %get-tuple-element.3), channel_id=1, replica_groups=mesh['list'=8,'shard'=4] {'list'}, dimensions={0}, use_global_device_ids=true | all-gather | bytes 147456 | tf_op jit(solution)/shard_map/all_gather | solution.py:34
  242.3 0.1 reshape.16
  242.4 1.1 fusion.2
  243.5 10.1 %all_to_all.39 = bf16[4,8,1024]{2,1,0:T(8,128)(2,1)S(1)} all-to-all(bf16[4,8,1024]{2,1,0:T(8,128)(2,1)S(1)} %fusion.2), channel_id=1, replica_groups=mesh['list'=8,'shard'=4] {'shard'}, dimensions={0} | all-to-all | bytes 131072 | tf_op jit(solution)/shard_map/all_to_all | solution.py:49
  253.6 0.6 copy.21
  (9 shorter events, 0.0 us)
Async XLA Ops:
  7.2 22.3 %copy-start = (bf16[1024,1376]{0,1:T(8,128)(2,1)S(1)}, bf16[1024,1376]{0,1:T(8,128)(2,1)}, u32[]{:S(2)}) copy-start(bf16[1024,1376]{0,1:T(8,128)(2,1)} %param.11) | copy-start | bytes 8454148
  7.2 94.6 %reduce-scatter.7.cloned.1.call-start = ((), (), s32[]{:S(2)}) async-start(), calls=%async_computation.5 | async-start | bytes 1802240 | tf_op jit(solution)/shard_map/reduce_scatter | solution.py:19
  7.2 23.2 %copy-start.4 = (bf16[1024,1376]{0,1:T(8,128)(2,1)S(1)}, bf16[1024,1376]{0,1:T(8,128)(2,1)}, u32[]{:S(2)}) copy-start(bf16[1024,1376]{0,1:T(8,128)(2,1)} %param.10) | copy-start | bytes 8454148
  32.5 2.6 %copy-start.2 = (s32[8]{0:T(128)S(1)}, s32[8]{0:T(128)}, u32[]{:S(2)}) copy-start(s32[8]{0:T(128)} %param.15) | copy-start | bytes 100
  32.5 2.7 %copy-start.3 = (s32[8]{0:T(128)S(1)}, s32[8]{0:T(128)}, u32[]{:S(2)}) copy-start(s32[8]{0:T(128)} %param.14) | copy-start | bytes 100
  35.1 119.1 %reduce-scatter.5.cloned.1.call-start = ((), (), s32[]{:S(2)}) async-start(), calls=%async_computation.4 | async-start | bytes 589824 | tf_op jit(solution)/shard_map/reduce_scatter | solution.py:26
  101.8 18.2 %copy-start.5 = (bf16[1376,1024]{1,0:T(8,128)(2,1)S(1)}, bf16[1376,1024]{1,0:T(8,128)(2,1)}, u32[]{:S(2)}) copy-start(bf16[1376,1024]{1,0:T(8,128)(2,1)} %param.12) | copy-start | bytes 8454148
  120.0 48.7 %copy-start.6 = (u32[32]{0:T(128)S(1)}, u32[32]{0:T(128)}, u32[]{:S(2)}) copy-start(u32[32]{0:T(128)} %constant.41) | copy-start | bytes 388
  120.0 113.1 %copy-start.1 = (f32[2,4096]{1,0:T(2,128)S(1)}, f32[2,4096]{1,0:T(2,128)}, u32[]{:S(2)}) copy-start(f32[2,4096]{1,0:T(2,128)} %param.13) | copy-start | bytes 98308
  121.8 97.4 %all-reduce.3.cloned.1.call-start = ((), (), s32[]{:S(2)}) async-start(), calls=%async_computation.6 | async-start | bytes 131072
Sparse Core Ops, SparseCore 0:
  35.2 31.2 reduce-scatter.6
  121.9 32.2 reduce-scatter.4
  168.7 50.4 all-reduce.2

commit v2 on v1

v2 whole, which is shorter than its diff:
```python
import functools

import jax
import jax.numpy as jnp
from jax import lax
from jax.experimental import pallas as pl
from jax.experimental.pallas import tpu as pltpu
from jax.sharding import PartitionSpec as P

MESH = pl.DeviceIdType.MESH
F32, BF16 = jnp.float32, jnp.bfloat16
FEAT, IDX, GATE, UP, HIDDEN, SQUARES, RESID, FRESH = range(8)
ROWS, IDX2, CENT, TERMS, SUMS = range(5)


def kernel(
    L, S,
    feat, gain, gate, up, down, cents, idx,
    out_res, out_fresh,
    gate_v, up_v, down_v, gain_v, cent_v, idx_v, group_v, rows_v,
    part_send, part_recv, hidden_v, term_send, term_recv, acc_v,
    square_v, res_send, res_recv, sum_send, sum_recv, fresh_v,
    local_sem, ss_sem, sr_sem, ls_sem, lr_sem,
):
    l, s = lax.axis_index("list"), lax.axis_index("shard")
    R, D = feat.shape
    C, G, N = D // S, R * S, R * S * L
    B = N // S
    own = cents.shape[0]
    per = L // S

    def cols(t):
        return pl.ds(pl.multiple_of(t * C, C), C)

    def block(t):
        return pl.ds(pl.multiple_of(t * B, B), B)

    def group(t):
        return pl.ds(pl.multiple_of(t * G, G), G)

    def shard_copy(kind, t, src, dst):
        return pltpu.make_async_remote_copy(
            src_ref=src, dst_ref=dst, send_sem=ss_sem.at[kind, t], recv_sem=sr_sem.at[kind, s],
            device_id={"shard": t}, device_id_type=MESH,
        )

    def shard_recv(kind, t, src, dst):
        pltpu.make_async_remote_copy(
            src_ref=src, dst_ref=dst, send_sem=ss_sem.at[kind, t], recv_sem=sr_sem.at[kind, t],
            device_id={"shard": t}, device_id_type=MESH,
        ).wait_recv()

    def list_copy(kind, t, src, dst):
        return pltpu.make_async_remote_copy(
            src_ref=src, dst_ref=dst, send_sem=ls_sem.at[kind, t], recv_sem=lr_sem.at[kind, l],
            device_id={"list": t}, device_id_type=MESH,
        )

    def list_recv(kind, t, src, dst):
        pltpu.make_async_remote_copy(
            src_ref=src, dst_ref=dst, send_sem=ls_sem.at[kind, t], recv_sem=lr_sem.at[kind, t],
            device_id={"list": t}, device_id_type=MESH,
        ).wait_recv()

    def others(n, me, body):
        @pl.loop(1, n)
        def _(i):
            body(lax.rem(me + i, n))

    locals_ = [
        pltpu.make_async_copy(gate, gate_v, local_sem.at[0]),
        pltpu.make_async_copy(up, up_v, local_sem.at[1]),
        pltpu.make_async_copy(down, down_v, local_sem.at[2]),
        pltpu.make_async_copy(gain.at[:, cols(s)], gain_v, local_sem.at[3]),
        pltpu.make_async_copy(cents.at[:, cols(s)], cent_v.at[l], local_sem.at[4]),
        pltpu.make_async_copy(idx, idx_v.at[l, s], local_sem.at[5]),
        pltpu.make_async_copy(feat.at[:, cols(s)], group_v.at[s], local_sem.at[6]),
    ]
    for copy in (locals_[6], locals_[5], locals_[0], locals_[1], locals_[2], locals_[3], locals_[4]):
        copy.start()

    barrier = pltpu.get_barrier_semaphore()
    others(S, s, lambda t: pl.semaphore_signal(barrier, inc=1, device_id={"shard": t}, device_id_type=MESH))
    others(L, l, lambda t: pl.semaphore_signal(barrier, inc=1, device_id={"list": t}, device_id_type=MESH))
    pl.semaphore_wait(barrier, S + L - 2)

    def send_features(t):
        shard_copy(FEAT, t, feat.at[:, cols(t)], group_v.at[s]).start()
        shard_copy(IDX, t, idx, idx_v.at[l, s]).start()

    others(S, s, send_features)
    others(L, l, lambda t: list_copy(CENT, t, cents.at[:, cols(s)], cent_v.at[l]).start())
    locals_[6].wait()
    locals_[5].wait()

    def recv_features(t):
        shard_recv(FEAT, t, feat.at[:, cols(t)], group_v.at[t])
        shard_recv(IDX, t, idx, idx_v.at[l, t])

    others(S, s, recv_features)
    mine = group_v[...].astype(F32).reshape(G, C)
    acc_v[...] = mine
    rows_v[group(l), :] = mine.astype(BF16)

    def send_rows(t):
        list_copy(ROWS, t, rows_v.at[group(l)], rows_v.at[group(l)]).start()

    others(L, l, send_rows)
    others(L, l, lambda t: list_copy(IDX2, t, idx_v.at[l], idx_v.at[l]).start())
    locals_[0].wait()
    locals_[1].wait()
    others(L, l, lambda t: list_recv(ROWS, t, rows_v.at[group(l)], rows_v.at[group(t)]))

    @pl.loop(1, S + 1)
    def _(i):
        t = lax.rem(s + i, S)
        a = rows_v[block(t), :]
        for kind, weight, k in ((GATE, gate_v, 0), (UP, up_v, 1)):
            part_send[k, t] = jnp.dot(a, weight[...], preferred_element_type=F32).astype(BF16)

            @pl.when(i < S)
            def _():
                shard_copy(kind, t, part_send.at[k, t], part_recv.at[k, s]).start()

    part_recv[0, s] = part_send[0, s]
    part_recv[1, s] = part_send[1, s]

    def recv_parts(t):
        shard_recv(GATE, t, part_send.at[0, t], part_recv.at[0, t])
        shard_recv(UP, t, part_send.at[1, t], part_recv.at[1, t])

    others(S, s, recv_parts)
    first = part_recv[0, 0].astype(F32)
    second = part_recv[1, 0].astype(F32)
    for j in range(1, S):
        first += part_recv[0, j].astype(F32)
        second += part_recv[1, j].astype(F32)
    hidden_v[block(s), :] = (first / (1.0 + jnp.exp(-first)) * second).astype(BF16)
    others(S, s, lambda t: shard_copy(HIDDEN, t, hidden_v.at[block(s)], hidden_v.at[block(s)]).start())

    locals_[2].wait()

    @pl.loop(0, S)
    def _(i):
        t = lax.rem(s + i, S)

        @pl.when(i > 0)
        def _():
            shard_recv(HIDDEN, t, hidden_v.at[block(s)], hidden_v.at[block(t)])

        term_send[block(t), :] = jnp.dot(
            hidden_v[block(t), :], down_v[...], preferred_element_type=F32
        ).astype(BF16)
        for j in range(per):
            g = t * per + j

            @pl.when(g != l)
            def _():
                list_copy(TERMS, g, term_send.at[group(g)], term_recv.at[l]).start()

    acc_v[...] += term_send[group(l), :].astype(F32)

    def add_term(t):
        list_recv(TERMS, t, term_send.at[group(t)], term_recv.at[t])
        acc_v[...] += term_recv[t].astype(F32)

    others(L, l, add_term)
    stream = acc_v[...]
    square_v[s] = jnp.broadcast_to(jnp.sum(stream * stream, axis=1, keepdims=True), (G, 128))
    others(S, s, lambda t: shard_copy(SQUARES, t, square_v.at[s], square_v.at[s]).start())

    for j in (3, 4):
        locals_[j].wait()

    def recv_small(t):
        list_recv(IDX2, t, idx_v.at[l], idx_v.at[t])
        list_recv(CENT, t, cents.at[:, cols(s)], cent_v.at[t])

    others(L, l, recv_small)
    mine_idx = idx_v[l].reshape(G, 256)
    ids, alive = mine_idx[:, :1], mine_idx[:, 128:129].astype(F32)
    coarse = jnp.zeros((G, C), F32)
    for g in range(L):
        for k in range(own):
            row = cent_v[g, k:k + 1, :].astype(BF16).astype(F32)
            coarse = coarse + jnp.where(ids == g * own + k, row, 0.0)
    every = idx_v[...].reshape(N, 256)
    counts = [
        jnp.sum(
            jnp.where(every[:, :128] == l * own + k, every[:, 128:].astype(F32), 0.0),
            axis=0, keepdims=True,
        )[:, :1]
        for k in range(own)
    ]

    others(S, s, lambda t: shard_recv(SQUARES, t, square_v.at[s], square_v.at[t]))
    squares = square_v[0]
    for j in range(1, S):
        squares = squares + square_v[j]
    scale = lax.rsqrt(squares[:, :1] / D + 1e-05)
    embedding = (acc_v[...] * scale * gain_v[...]).astype(BF16).astype(F32)
    weighted = alive * embedding
    for g in range(L):
        for k in range(own):
            sum_send[g, k:k + 1, :] = jnp.sum(
                jnp.where(ids == g * own + k, weighted, 0.0), axis=0, keepdims=True
            )
    others(L, l, lambda t: list_copy(SUMS, t, sum_send.at[t], sum_recv.at[l]).start())
    res_send[...] = (alive * (embedding - coarse)).reshape(S, R, C).astype(BF16)
    others(S, s, lambda t: shard_copy(RESID, t, res_send.at[t], res_recv.at[s]).start())
    res_recv[s] = res_send[s]
    sum_recv[l] = sum_send[l]
    others(L, l, lambda t: list_recv(SUMS, t, sum_send.at[t], sum_recv.at[t]))
    for k in range(own):
        total = cent_v[l, k:k + 1, :]
        for g in range(L):
            total = total + sum_recv[g, k:k + 1, :]
        fresh_v[s, k:k + 1, :] = total / (1.0 + counts[k])
    others(S, s, lambda t: shard_copy(FRESH, t, fresh_v.at[s], fresh_v.at[s]).start())
    others(S, s, lambda t: shard_recv(RESID, t, res_send.at[t], res_recv.at[t]))
    for j in range(S):
        out_res[:, j * C:(j + 1) * C] = res_recv[j]
    others(S, s, lambda t: shard_recv(FRESH, t, fresh_v.at[s], fresh_v.at[t]))
    for j in range(S):
        out_fresh[:, j * C:(j + 1) * C] = fresh_v[j]

    def shard_sent(t):
        shard_copy(FEAT, t, feat.at[:, cols(t)], group_v.at[s]).wait_send()
        shard_copy(IDX, t, idx, idx_v.at[l, s]).wait_send()
        shard_copy(GATE, t, part_send.at[0, t], part_recv.at[0, s]).wait_send()
        shard_copy(UP, t, part_send.at[1, t], part_recv.at[1, s]).wait_send()
        shard_copy(HIDDEN, t, hidden_v.at[block(s)], hidden_v.at[block(s)]).wait_send()
        shard_copy(SQUARES, t, square_v.at[s], square_v.at[s]).wait_send()
        shard_copy(RESID, t, res_send.at[t], res_recv.at[s]).wait_send()
        shard_copy(FRESH, t, fresh_v.at[s], fresh_v.at[s]).wait_send()

    others(S, s, shard_sent)

    def list_sent(t):
        list_copy(ROWS, t, rows_v.at[group(l)], rows_v.at[group(l)]).wait_send()
        list_copy(IDX2, t, idx_v.at[l], idx_v.at[l]).wait_send()
        list_copy(CENT, t, cents.at[:, cols(s)], cent_v.at[l]).wait_send()
        list_copy(TERMS, t, term_send.at[group(t)], term_recv.at[l]).wait_send()
        list_copy(SUMS, t, sum_send.at[t], sum_recv.at[l]).wait_send()

    others(L, l, list_sent)


def solution(mesh):
    L, S = mesh.shape["list"], mesh.shape["shard"]

    def body(features, norm_gain, gate_weight, up_weight, down_weight, centroids, list_ids, live):
        R, D = features.shape
        C, F = gate_weight.shape
        own = centroids.shape[0]
        G, N = R * S, R * S * L
        B = N // S
        packed = jnp.concatenate(
            [jnp.broadcast_to(v[:, None], (R, 128)) for v in (list_ids, live)], axis=1
        )
        return pl.pallas_call(
            functools.partial(kernel, L, S),
            out_shape=(
                jax.ShapeDtypeStruct((R, D), BF16),
                jax.ShapeDtypeStruct((own, D), F32),
            ),
            in_specs=[pl.BlockSpec(memory_space=pl.ANY)] * 7,
            out_specs=[pl.BlockSpec(memory_space=pltpu.VMEM)] * 2,
            scratch_shapes=[
                pltpu.VMEM((C, F), BF16),
                pltpu.VMEM((C, F), BF16),
                pltpu.VMEM((F, C), BF16),
                pltpu.VMEM((1, C), F32),
                pltpu.VMEM((L, own, C), F32),
                pltpu.VMEM((L, S, R, 256), jnp.int32),
                pltpu.VMEM((S, R, C), BF16),
                pltpu.VMEM((N, C), BF16),
                pltpu.VMEM((2, S, B, F), BF16),
                pltpu.VMEM((2, S, B, F), BF16),
                pltpu.VMEM((N, F), BF16),
                pltpu.VMEM((N, C), BF16),
                pltpu.VMEM((L, G, C), BF16),
                pltpu.VMEM((G, C), F32),
                pltpu.VMEM((S, G, 128), F32),
                pltpu.VMEM((S, R, C), BF16),
                pltpu.VMEM((S, R, C), BF16),
                pltpu.VMEM((L, own, C), F32),
                pltpu.VMEM((L, own, C), F32),
                pltpu.VMEM((S, own, C), F32),
                pltpu.SemaphoreType.DMA((7,)),
                pltpu.SemaphoreType.DMA((8, S)),
                pltpu.SemaphoreType.DMA((8, S)),
                pltpu.SemaphoreType.DMA((5, L)),
                pltpu.SemaphoreType.DMA((5, L)),
            ],
            compiler_params=pltpu.CompilerParams(collective_id=0, has_side_effects=True),
        )(features, norm_gain[None, :], gate_weight, up_weight, down_weight, centroids, packed)

    in_specs = (
        P(("list", "shard"), None),
        P(),
        P("shard", "list"),
        P("shard", "list"),
        P("list", "shard"),
        P("list", None),
        P(("list", "shard")),
        P(("list", "shard")),
    )
    out_specs = (P(("list", "shard"), None), P("list", None))
    return jax.shard_map(body, mesh=mesh, in_specs=in_specs, out_specs=out_specs, check_vma=False)
```

time: 261 us -> 101 us (0.39)
  blocking collectives: 148 us -> 0 us
  Pallas kernels: 0 us -> 87.6 us
  waiting for transfers between devices: 81.4 us -> 0 us
  between operations: 14.5 us -> 0.64 us
  matrix products: 6.43 us -> 0 us
  local copies, waits for them, and re-layouts: 5.48 us -> 11.9 us
  other arithmetic: 4.43 us -> 0.6 us
    all_gather x5 -> x0, blocking collectives: 114 us -> none  [the longest x1 65.8 us: body(): lax.all_gather(jnp.stack([list_ids, live], axis=1), ('list', 'shard'), ax...]
    pallas_call x0 -> x1, Pallas kernels: none -> 87.6 us  [body(): pl.pallas_call(functools.partial(kernel, L, S), out_shape=(jax.ShapeDtype...]
    unnamed x4 -> x0, waiting for transfers between devices: 49.3 us -> none
    reduce_scatter x2 -> x0, waiting for transfers between devices: 32.1 us -> none  [the longest x1 32.1 us: body(): lax.psum_scatter(terms.astype(jnp.bfloat16), 'list', scatter_dimension=0,...]
    all_to_all x2 -> x0, blocking collectives: 22.5 us -> none  [the longest x1 12.4 us: body(): lax.all_to_all(features, 'shard', split_axis=1, concat_axis=0, tiled=True)]
    psum x1 -> x0, blocking collectives: 11.7 us -> none  [body(): squares = lax.psum(jnp.sum(stream * stream, axis=1, keepdims=True), 'shard')]
    dot_general x5 -> x0, matrix products: 6.43 us -> none  [the longest x1 1.77 us: body(): terms = jnp.dot(hidden, down_weight, preferred_element_type=jnp.float32)]
    unnamed x20 -> x6, local copies, waits for them, and re-layouts: 4.71 us -> 10.4 us
  transfers between devices with their start and end apart: 3 -> 0, of which waited for: 2 -> 0; matrix products, arithmetic and copies ran while one was open for 1% -> 0% of each run, Pallas kernels for 0% -> 0%
where the time goes in v2:
time: 101 us
  Pallas kernels  87.6 us (87%)
  local copies, waits for them, and re-layouts  11.9 us (12%)
    pallas_call x1, Pallas kernels, body(): pl.pallas_call(functools.partial(kernel, L, S), out_shape=(jax.ShapeDtype...  87.6 us
    unnamed x6, local copies, waits for them, and re-layouts  10.4 us

profile of v2, /device:TPU:0, one launch (start us, length us, event | category | flops | bytes accessed | tf_op | source)
XLA Modules:
  0.0 100.7 jit_solution(6810303788272256156)
XLA Ops:
  0.6 0.7 broadcast_in_dim.7
  1.4 0.7 broadcast_in_dim.8
  2.1 0.6 pad_add_fusion.idx
  2.7 0.0 copy-start
  2.7 4.7 %copy.10.gate = bf16[1024,1376]{1,0:T(8,128)(2,1)} copy(bf16[1024,1376]{0,1:T(8,128)(2,1)} %param.10) | data formatting | bytes 5636096 | tf_op args[2]
  7.4 0.0 copy-done
  7.4 2.9 %copy.11.up = bf16[1024,1376]{1,0:T(8,128)(2,1)} copy(bf16[1024,1376]{0,1:T(8,128)(2,1)S(1)} %copy-done) | data formatting | bytes 5636096 | tf_op args[3]
  10.3 87.6 %shard_map.95 = (bf16[8,4096]{1,0:T(8,128)(2,1)}, f32[2,4096]{1,0:T(2,128)}) custom-call(bf16[8,4096]{1,0:T(8,128)(2,1)} %feat.1, f32[1,4096]{1,0:T(1,128)} %bitcast.1, bf16[1024,1376]{1,0:T(8,128)(2,1)} %copy.10.gate, bf16[1024,1376]{1,0:T(8,128)(2,1)} %copy.11.up, bf16[1376,1024]{1,0:T(8,128)(2,1)} %down.1, f32[2,4096]{1,0:T(2,128)} %cents.1, ...), custom_call_target="tpu_custom_call" | custom-call | tf_op jit(solution)/shard_map/pallas_call | solution.py:261
  97.8 1.5 %copy.14 = bf16[8,4096]{1,0:T(8,128)(2,1)} copy(bf16[8,4096]{1,0:T(8,128)(2,1)} %get-tuple-element.4) | data formatting | bytes 131072
  99.3 1.4 %copy.15 = f32[2,4096]{1,0:T(2,128)} copy(f32[2,4096]{1,0:T(2,128)} %get-tuple-element.5) | data formatting | bytes 65536
Async XLA Ops:
  2.7 4.7 %copy-start = (bf16[1024,1376]{0,1:T(8,128)(2,1)S(1)}, bf16[1024,1376]{0,1:T(8,128)(2,1)}, u32[]{:S(2)}) copy-start(bf16[1024,1376]{0,1:T(8,128)(2,1)} %param.11) | copy-start | bytes 8454148

commit v3 on v2

--- a/solution.py
+++ b/solution.py
@@ -71,7 +71,7 @@
         pltpu.make_async_copy(gate, gate_v, local_sem.at[0]),
         pltpu.make_async_copy(up, up_v, local_sem.at[1]),
         pltpu.make_async_copy(down, down_v, local_sem.at[2]),
-        pltpu.make_async_copy(gain.at[:, cols(s)], gain_v, local_sem.at[3]),
+        pltpu.make_async_copy(gain.at[cols(s)], gain_v.at[0], local_sem.at[3]),
         pltpu.make_async_copy(cents.at[:, cols(s)], cent_v.at[l], local_sem.at[4]),
         pltpu.make_async_copy(idx, idx_v.at[l, s], local_sem.at[5]),
         pltpu.make_async_copy(feat.at[:, cols(s)], group_v.at[s], local_sem.at[6]),
@@ -116,7 +116,9 @@
         t = lax.rem(s + i, S)
         a = rows_v[block(t), :]
         for kind, weight, k in ((GATE, gate_v, 0), (UP, up_v, 1)):
-            part_send[k, t] = jnp.dot(a, weight[...], preferred_element_type=F32).astype(BF16)
+            part_send[k, t] = lax.dot_general(
+                a, weight[...], (((1,), (1,)), ((), ())), preferred_element_type=F32
+            ).astype(BF16)
 
             @pl.when(i < S)
             def _():
@@ -255,9 +257,8 @@
         own = centroids.shape[0]
         G, N = R * S, R * S * L
         B = N // S
-        packed = jnp.concatenate(
-            [jnp.broadcast_to(v[:, None], (R, 128)) for v in (list_ids, live)], axis=1
-        )
+        lane = lax.broadcasted_iota(jnp.int32, (R, 256), 1)
+        packed = jnp.where(lane < 128, list_ids[:, None], live[:, None])
         return pl.pallas_call(
             functools.partial(kernel, L, S),
             out_shape=(
@@ -267,8 +268,8 @@
             in_specs=[pl.BlockSpec(memory_space=pl.ANY)] * 7,
             out_specs=[pl.BlockSpec(memory_space=pltpu.VMEM)] * 2,
             scratch_shapes=[
-                pltpu.VMEM((C, F), BF16),
-                pltpu.VMEM((C, F), BF16),
+                pltpu.VMEM((F, C), BF16),
+                pltpu.VMEM((F, C), BF16),
                 pltpu.VMEM((F, C), BF16),
                 pltpu.VMEM((1, C), F32),
                 pltpu.VMEM((L, own, C), F32),
@@ -294,7 +295,7 @@
                 pltpu.SemaphoreType.DMA((5, L)),
             ],
             compiler_params=pltpu.CompilerParams(collective_id=0, has_side_effects=True),
-        )(features, norm_gain[None, :], gate_weight, up_weight, down_weight, centroids, packed)
+        )(features, norm_gain, gate_weight.T, up_weight.T, down_weight, centroids, packed)
 
     in_specs = (
         P(("list", "shard"), None),

time: 101 us -> 93 us (0.921)
  local copies, waits for them, and re-layouts: 11.9 us -> 2.85 us
    unnamed x6 -> x2, local copies, waits for them, and re-layouts: 10.4 us -> 2.85 us
    broadcast_in_dim x2 -> x0, local copies, waits for them, and re-layouts: 1.45 us -> none  [body(): jnp.broadcast_to(v[:, None], (R, 128))]
    select_n x0 -> x1, other arithmetic: none -> 1.34 us  [body(): packed = jnp.where(lane < 128, list_ids[:, None], live[:, None])]
where the time goes in v3:
time: 93 us; the launch traced here: 92.8 us
  Pallas kernels  88 us (95%)
  local copies, waits for them, and re-layouts  2.85 us (3%)
  other arithmetic  1.35 us (1%)
    pallas_call x1, Pallas kernels, body(): pl.pallas_call(functools.partial(kernel, L, S), out_shape=(jax.ShapeDtype...  88 us
    unnamed x2, local copies, waits for them, and re-layouts  2.85 us

profile of v3, /device:TPU:0, one launch (start us, length us, event | category | flops | bytes accessed | tf_op | source)
XLA Modules:
  0.0 92.8 jit_solution(4886396022480454073)
XLA Ops:
  0.6 1.3 %broadcast_select_fusion.idx = s32[8,256]{1,0:T(8,128)} fusion(s32[8]{0:T(128)} %param.15, s32[8]{0:T(128)} %param.14, pred[256]{0:T(512)(128)(4,1)S(1)} %iota_compare_fusion), kind=kLoop, calls=%fused_computation | loop fusion | flops 2048 | bytes 8512 | tf_op jit(solution)/shard_map/jit(_where)/select_n | solution.py:261
  2.0 88.0 %shard_map.95 = (bf16[8,4096]{1,0:T(8,128)(2,1)}, f32[2,4096]{1,0:T(2,128)}) custom-call(bf16[8,4096]{1,0:T(8,128)(2,1)} %feat.1, f32[4096]{0:T(1024)} %gain.1, bf16[1376,1024]{1,0:T(8,128)(2,1)} %bitcast.2, bf16[1376,1024]{1,0:T(8,128)(2,1)} %bitcast.3, bf16[1376,1024]{1,0:T(8,128)(2,1)} %down.1, f32[2,4096]{1,0:T(2,128)} %cents.1, ...), custom_call_target="tpu_custom_call" | custom-call | tf_op jit(solution)/shard_map/pallas_call | solution.py:262
  90.0 1.5 %copy.12 = bf16[8,4096]{1,0:T(8,128)(2,1)} copy(bf16[8,4096]{1,0:T(8,128)(2,1)} %get-tuple-element.4) | data formatting | bytes 131072
  91.4 1.4 %copy.13 = f32[2,4096]{1,0:T(2,128)} copy(f32[2,4096]{1,0:T(2,128)} %get-tuple-element.5) | data formatting | bytes 65536
  (1 shorter events, 0.0 us)

commit v4 on v3

--- a/solution.py
+++ b/solution.py
@@ -9,7 +9,7 @@
 
 MESH = pl.DeviceIdType.MESH
 F32, BF16 = jnp.float32, jnp.bfloat16
-FEAT, IDX, GATE, UP, HIDDEN, SQUARES, RESID, FRESH = range(8)
+FEAT, IDX, SQUARES, RESID, FRESH = range(5)
 ROWS, IDX2, CENT, TERMS, SUMS = range(5)
 
 
@@ -18,22 +18,19 @@
     feat, gain, gate, up, down, cents, idx,
     out_res, out_fresh,
     gate_v, up_v, down_v, gain_v, cent_v, idx_v, group_v, rows_v,
-    part_send, part_recv, hidden_v, term_send, term_recv, acc_v,
+    part_v, part_recv, hidden_v, term_send, term_recv, acc_v,
     square_v, res_send, res_recv, sum_send, sum_recv, fresh_v,
-    local_sem, ss_sem, sr_sem, ls_sem, lr_sem,
+    local_sem, ss_sem, sr_sem, ls_sem, lr_sem, cs_sem, cr_sem, bs_sem, br_sem,
 ):
     l, s = lax.axis_index("list"), lax.axis_index("shard")
     R, D = feat.shape
     C, G, N = D // S, R * S, R * S * L
-    B = N // S
+    H = N // 2
+    K, ck = L, G // 2
     own = cents.shape[0]
-    per = L // S
 
     def cols(t):
         return pl.ds(pl.multiple_of(t * C, C), C)
-
-    def block(t):
-        return pl.ds(pl.multiple_of(t * B, B), B)
 
     def group(t):
         return pl.ds(pl.multiple_of(t * G, G), G)
@@ -111,54 +108,100 @@
     locals_[1].wait()
     others(L, l, lambda t: list_recv(ROWS, t, rows_v.at[group(l)], rows_v.at[group(t)]))
 
-    @pl.loop(1, S + 1)
+    M = min(H, 4 * G)
+
+    def chain_copy(h, k, t):
+        return pltpu.make_async_remote_copy(
+            src_ref=part_v.at[h, k], dst_ref=part_recv.at[h, k],
+            send_sem=cs_sem.at[h, k], recv_sem=cr_sem.at[h, k],
+            device_id={"shard": t}, device_id_type=MESH,
+        )
+
+    def chunk(h, k):
+        return pl.ds(pl.multiple_of((h * K + k) * ck, ck), ck)
+
+    def back_copy(h, k, t):
+        return pltpu.make_async_remote_copy(
+            src_ref=hidden_v.at[chunk(h, k)], dst_ref=hidden_v.at[chunk(h, k)],
+            send_sem=bs_sem.at[h, k], recv_sem=br_sem.at[h, k],
+            device_id={"shard": t}, device_id_type=MESH,
+        )
+
+    def place(h):
+        return h * s + (1 - h) * (S - 1 - s), s + (2 * h - 1), s - (2 * h - 1)
+
+    early = 1 - s // max(S // 2, 1)
+
+    @pl.loop(0, 2)
     def _(i):
-        t = lax.rem(s + i, S)
-        a = rows_v[block(t), :]
-        for kind, weight, k in ((GATE, gate_v, 0), (UP, up_v, 1)):
-            part_send[k, t] = lax.dot_general(
-                a, weight[...], (((1,), (1,)), ((), ())), preferred_element_type=F32
+        h = lax.rem(early + i, 2)
+        p, nxt, prv = place(h)
+
+        @pl.loop(0, H // M)
+        def _(b):
+            a = rows_v[pl.ds(pl.multiple_of(h * H + b * M, M), M), :]
+            for j, weight in ((0, gate_v), (1, up_v)):
+                product = lax.dot_general(
+                    a, weight[...], (((1,), (1,)), ((), ())), preferred_element_type=F32
+                ).astype(BF16)
+                for c in range(M // ck):
+                    part_v[h, b * (M // ck) + c, j] = product[c * ck:(c + 1) * ck, :]
+
+        @pl.when(p == 0)
+        def _():
+            @pl.loop(0, K)
+            def _(k):
+                chain_copy(h, k, nxt).start()
+
+    locals_[2].wait()
+
+    def finish(h, k):
+        @pl.when(lax.rem(k, 2) == 1)
+        def _():
+            g = h * (L // 2) + k // 2
+            term_send[group(g), :] = jnp.dot(
+                hidden_v[group(g), :], down_v[...], preferred_element_type=F32
             ).astype(BF16)
 
-            @pl.when(i < S)
-            def _():
-                shard_copy(kind, t, part_send.at[k, t], part_recv.at[k, s]).start()
-
-    part_recv[0, s] = part_send[0, s]
-    part_recv[1, s] = part_send[1, s]
-
-    def recv_parts(t):
-        shard_recv(GATE, t, part_send.at[0, t], part_recv.at[0, t])
-        shard_recv(UP, t, part_send.at[1, t], part_recv.at[1, t])
-
-    others(S, s, recv_parts)
-    first = part_recv[0, 0].astype(F32)
-    second = part_recv[1, 0].astype(F32)
-    for j in range(1, S):
-        first += part_recv[0, j].astype(F32)
-        second += part_recv[1, j].astype(F32)
-    hidden_v[block(s), :] = (first / (1.0 + jnp.exp(-first)) * second).astype(BF16)
-    others(S, s, lambda t: shard_copy(HIDDEN, t, hidden_v.at[block(s)], hidden_v.at[block(s)]).start())
-
-    locals_[2].wait()
-
-    @pl.loop(0, S)
-    def _(i):
-        t = lax.rem(s + i, S)
-
-        @pl.when(i > 0)
-        def _():
-            shard_recv(HIDDEN, t, hidden_v.at[block(s)], hidden_v.at[block(t)])
-
-        term_send[block(t), :] = jnp.dot(
-            hidden_v[block(t), :], down_v[...], preferred_element_type=F32
-        ).astype(BF16)
-        for j in range(per):
-            g = t * per + j
-
             @pl.when(g != l)
             def _():
                 list_copy(TERMS, g, term_send.at[group(g)], term_recv.at[l]).start()
+
+    @pl.loop(0, 6 * (S - 1) + K)
+    def _(step):
+        @pl.loop(0, 2)
+        def _(h):
+            p, nxt, prv = place(h)
+            k = step - 3 * p
+
+            @pl.when((p > 0) & (k >= 0) & (k < K))
+            def _():
+                chain_copy(h, k, prv).wait_recv()
+
+                @pl.when(p < S - 1)
+                def _():
+                    part_v[h, k] = (part_v[h, k].astype(F32) + part_recv[h, k].astype(F32)).astype(BF16)
+                    chain_copy(h, k, nxt).start()
+
+                @pl.when(p == S - 1)
+                def _():
+                    first = part_v[h, k, 0].astype(F32) + part_recv[h, k, 0].astype(F32)
+                    second = part_v[h, k, 1].astype(F32) + part_recv[h, k, 1].astype(F32)
+                    hidden_v[chunk(h, k), :] = (first / (1.0 + jnp.exp(-first)) * second).astype(BF16)
+                    back_copy(h, k, prv).start()
+                    finish(h, k)
+
+            q = step - 3 * (S - 1) - 3 * (S - 1 - p)
+
+            @pl.when((p < S - 1) & (q >= 0) & (q < K))
+            def _():
+                back_copy(h, q, nxt).wait_recv()
+
+                @pl.when(p > 0)
+                def _():
+                    back_copy(h, q, prv).start()
+
+                finish(h, q)
 
     acc_v[...] += term_send[group(l), :].astype(F32)
 
@@ -229,9 +272,6 @@
     def shard_sent(t):
         shard_copy(FEAT, t, feat.at[:, cols(t)], group_v.at[s]).wait_send()
         shard_copy(IDX, t, idx, idx_v.at[l, s]).wait_send()
-        shard_copy(GATE, t, part_send.at[0, t], part_recv.at[0, s]).wait_send()
-        shard_copy(UP, t, part_send.at[1, t], part_recv.at[1, s]).wait_send()
-        shard_copy(HIDDEN, t, hidden_v.at[block(s)], hidden_v.at[block(s)]).wait_send()
         shard_copy(SQUARES, t, square_v.at[s], square_v.at[s]).wait_send()
         shard_copy(RESID, t, res_send.at[t], res_recv.at[s]).wait_send()
         shard_copy(FRESH, t, fresh_v.at[s], fresh_v.at[s]).wait_send()
@@ -247,6 +287,20 @@
 
     others(L, l, list_sent)
 
+    @pl.loop(0, 2)
+    def _(h):
+        p, nxt, prv = place(h)
+
+        @pl.loop(0, K)
+        def _(k):
+            @pl.when(p < S - 1)
+            def _():
+                chain_copy(h, k, nxt).wait_send()
+
+            @pl.when(p > 0)
+            def _():
+                back_copy(h, k, prv).wait_send()
+
 
 def solution(mesh):
     L, S = mesh.shape["list"], mesh.shape["shard"]
@@ -256,7 +310,6 @@
         C, F = gate_weight.shape
         own = centroids.shape[0]
         G, N = R * S, R * S * L
-        B = N // S
         lane = lax.broadcasted_iota(jnp.int32, (R, 256), 1)
         packed = jnp.where(lane < 128, list_ids[:, None], live[:, None])
         return pl.pallas_call(
@@ -276,8 +329,8 @@
                 pltpu.VMEM((L, S, R, 256), jnp.int32),
                 pltpu.VMEM((S, R, C), BF16),
                 pltpu.VMEM((N, C), BF16),
-                pltpu.VMEM((2, S, B, F), BF16),
-                pltpu.VMEM((2, S, B, F), BF16),
+                pltpu.VMEM((2, L, 2, G // 2, F), BF16),
+                pltpu.VMEM((2, L, 2, G // 2, F), BF16),
                 pltpu.VMEM((N, F), BF16),
                 pltpu.VMEM((N, C), BF16),
                 pltpu.VMEM((L, G, C), BF16),
@@ -289,10 +342,14 @@
                 pltpu.VMEM((L, own, C), F32),
                 pltpu.VMEM((S, own, C), F32),
                 pltpu.SemaphoreType.DMA((7,)),
-                pltpu.SemaphoreType.DMA((8, S)),
-                pltpu.SemaphoreType.DMA((8, S)),
+                pltpu.SemaphoreType.DMA((5, S)),
+                pltpu.SemaphoreType.DMA((5, S)),
                 pltpu.SemaphoreType.DMA((5, L)),
                 pltpu.SemaphoreType.DMA((5, L)),
+                pltpu.SemaphoreType.DMA((2, L)),
+                pltpu.SemaphoreType.DMA((2, L)),
+                pltpu.SemaphoreType.DMA((2, L)),
+                pltpu.SemaphoreType.DMA((2, L)),
             ],
             compiler_params=pltpu.CompilerParams(collective_id=0, has_side_effects=True),
         )(features, norm_gain, gate_weight.T, up_weight.T, down_weight, centroids, packed)

time: 93 us -> 78.9 us (0.85)
  Pallas kernels: 88 us -> 73.8 us
    pallas_call x1, Pallas kernels: 88 us -> 73.8 us  [body(): pl.pallas_call(functools.partial(kernel, L, S), out_shape=(jax.ShapeDtype...]
where the time goes in v4:
time: 78.9 us; the launch traced here: 78.7 us
  Pallas kernels  73.8 us (94%)
  local copies, waits for them, and re-layouts  2.85 us (4%)
  other arithmetic  1.35 us (2%)
    pallas_call x1, Pallas kernels, body(): pl.pallas_call(functools.partial(kernel, L, S), out_shape=(jax.ShapeDtype...  73.8 us
    unnamed x2, local copies, waits for them, and re-layouts  2.85 us

profile of v4, /device:TPU:0, one launch (start us, length us, event | category | flops | bytes accessed | tf_op | source)
XLA Modules:
  0.0 78.7 jit_solution(13471512543836847735)
XLA Ops:
  0.6 1.3 %broadcast_select_fusion.idx = s32[8,256]{1,0:T(8,128)} fusion(s32[8]{0:T(128)} %param.15, s32[8]{0:T(128)} %param.14, pred[256]{0:T(512)(128)(4,1)S(1)} %iota_compare_fusion), kind=kLoop, calls=%fused_computation | loop fusion | flops 2048 | bytes 8512 | tf_op jit(solution)/shard_map/jit(_where)/select_n | solution.py:314
  2.0 73.8 %shard_map.95 = (bf16[8,4096]{1,0:T(8,128)(2,1)}, f32[2,4096]{1,0:T(2,128)}) custom-call(bf16[8,4096]{1,0:T(8,128)(2,1)} %feat.1, f32[4096]{0:T(1024)} %gain.1, bf16[1376,1024]{1,0:T(8,128)(2,1)} %bitcast.2, bf16[1376,1024]{1,0:T(8,128)(2,1)} %bitcast.3, bf16[1376,1024]{1,0:T(8,128)(2,1)} %down.1, f32[2,4096]{1,0:T(2,128)} %cents.1, ...), custom_call_target="tpu_custom_call" | custom-call | tf_op jit(solution)/shard_map/pallas_call | solution.py:315
  75.8 1.5 %copy.12 = bf16[8,4096]{1,0:T(8,128)(2,1)} copy(bf16[8,4096]{1,0:T(8,128)(2,1)} %get-tuple-element.4) | data formatting | bytes 131072
  77.3 1.4 %copy.13 = f32[2,4096]{1,0:T(2,128)} copy(f32[2,4096]{1,0:T(2,128)} %get-tuple-element.5) | data formatting | bytes 65536
  (1 shorter events, 0.0 us)

commit v5 on v4

--- a/solution.py
+++ b/solution.py
@@ -10,7 +10,7 @@
 MESH = pl.DeviceIdType.MESH
 F32, BF16 = jnp.float32, jnp.bfloat16
 FEAT, IDX, SQUARES, RESID, FRESH = range(5)
-ROWS, IDX2, CENT, TERMS, SUMS = range(5)
+ROWS, IDX2, CENT, TERMS, SUMS, PASSED = range(6)
 
 
 def kernel(
@@ -102,11 +102,33 @@
     def send_rows(t):
         list_copy(ROWS, t, rows_v.at[group(l)], rows_v.at[group(l)]).start()
 
-    others(L, l, send_rows)
+    mate = l + 1 - 2 * lax.rem(l, 2)
+
+    def peers(me, body):
+        @pl.loop(1, L // 2)
+        def _(i):
+            body(lax.rem(me + 2 * i, L))
+
+    peers(l, send_rows)
+    send_rows(mate)
     others(L, l, lambda t: list_copy(IDX2, t, idx_v.at[l], idx_v.at[l]).start())
     locals_[0].wait()
     locals_[1].wait()
-    others(L, l, lambda t: list_recv(ROWS, t, rows_v.at[group(l)], rows_v.at[group(t)]))
+
+    def pass_on(t):
+        return pltpu.make_async_remote_copy(
+            src_ref=rows_v.at[group(t)], dst_ref=rows_v.at[group(t)],
+            send_sem=ls_sem.at[PASSED, t], recv_sem=lr_sem.at[PASSED, t],
+            device_id={"list": mate}, device_id_type=MESH,
+        )
+
+    def relay_rows(t):
+        list_recv(ROWS, t, rows_v.at[group(l)], rows_v.at[group(t)])
+        pass_on(t).start()
+
+    peers(l, relay_rows)
+    list_recv(ROWS, mate, rows_v.at[group(l)], rows_v.at[group(mate)])
+    peers(mate, lambda t: pass_on(t).wait_recv())
 
     M = min(H, 4 * G)
 
@@ -279,13 +301,19 @@
     others(S, s, shard_sent)
 
     def list_sent(t):
-        list_copy(ROWS, t, rows_v.at[group(l)], rows_v.at[group(l)]).wait_send()
         list_copy(IDX2, t, idx_v.at[l], idx_v.at[l]).wait_send()
         list_copy(CENT, t, cents.at[:, cols(s)], cent_v.at[l]).wait_send()
         list_copy(TERMS, t, term_send.at[group(t)], term_recv.at[l]).wait_send()
         list_copy(SUMS, t, sum_send.at[t], sum_recv.at[l]).wait_send()
 
     others(L, l, list_sent)
+
+    def rows_sent(t):
+        list_copy(ROWS, t, rows_v.at[group(l)], rows_v.at[group(l)]).wait_send()
+
+    peers(l, rows_sent)
+    rows_sent(mate)
+    peers(l, lambda t: pass_on(t).wait_send())
 
     @pl.loop(0, 2)
     def _(h):
@@ -344,8 +372,8 @@
                 pltpu.SemaphoreType.DMA((7,)),
                 pltpu.SemaphoreType.DMA((5, S)),
                 pltpu.SemaphoreType.DMA((5, S)),
-                pltpu.SemaphoreType.DMA((5, L)),
-                pltpu.SemaphoreType.DMA((5, L)),
+                pltpu.SemaphoreType.DMA((6, L)),
+                pltpu.SemaphoreType.DMA((6, L)),
                 pltpu.SemaphoreType.DMA((2, L)),
                 pltpu.SemaphoreType.DMA((2, L)),
                 pltpu.SemaphoreType.DMA((2, L)),

time: 78.9 us -> 76.2 us (0.966)
  Pallas kernels: 73.8 us -> 71.1 us
    pallas_call x1, Pallas kernels: 73.8 us -> 71.1 us  [body(): pl.pallas_call(functools.partial(kernel, L, S), out_shape=(jax.ShapeDtype...]
where the time goes in v5:
time: 76.2 us; the launch traced here: 75.9 us
  Pallas kernels  71.1 us (93%)
  local copies, waits for them, and re-layouts  2.85 us (4%)
  other arithmetic  1.35 us (2%)
    pallas_call x1, Pallas kernels, body(): pl.pallas_call(functools.partial(kernel, L, S), out_shape=(jax.ShapeDtype...  71.1 us
    unnamed x2, local copies, waits for them, and re-layouts  2.85 us

profile of v5, /device:TPU:0, one launch (start us, length us, event | category | flops | bytes accessed | tf_op | source)
XLA Modules:
  0.0 75.9 jit_solution(9365057496754027776)
XLA Ops:
  0.6 1.3 %broadcast_select_fusion.idx = s32[8,256]{1,0:T(8,128)} fusion(s32[8]{0:T(128)} %param.15, s32[8]{0:T(128)} %param.14, pred[256]{0:T(512)(128)(4,1)S(1)} %iota_compare_fusion), kind=kLoop, calls=%fused_computation | loop fusion | flops 2048 | bytes 8512 | tf_op jit(solution)/shard_map/jit(_where)/select_n | solution.py:342
  2.0 71.1 %shard_map.95 = (bf16[8,4096]{1,0:T(8,128)(2,1)}, f32[2,4096]{1,0:T(2,128)}) custom-call(bf16[8,4096]{1,0:T(8,128)(2,1)} %feat.1, f32[4096]{0:T(1024)} %gain.1, bf16[1376,1024]{1,0:T(8,128)(2,1)} %bitcast.2, bf16[1376,1024]{1,0:T(8,128)(2,1)} %bitcast.3, bf16[1376,1024]{1,0:T(8,128)(2,1)} %down.1, f32[2,4096]{1,0:T(2,128)} %cents.1, ...), custom_call_target="tpu_custom_call" | custom-call | tf_op jit(solution)/shard_map/pallas_call | solution.py:343
  73.1 1.5 %copy.12 = bf16[8,4096]{1,0:T(8,128)(2,1)} copy(bf16[8,4096]{1,0:T(8,128)(2,1)} %get-tuple-element.4) | data formatting | bytes 131072
  74.6 1.4 %copy.13 = f32[2,4096]{1,0:T(2,128)} copy(f32[2,4096]{1,0:T(2,128)} %get-tuple-element.5) | data formatting | bytes 65536
  (1 shorter events, 0.0 us)
